TPU v7x, 128 devices: a whole 4x4x4 slice. The times are simulated.
128 devices in a mesh: seq: 32 (over z, y, core), tp: 4 (over x).
Axes of the slice: x: 4, y: 4, z: 4, core: 2. Of those that a mesh axis runs over, the one named last changes fastest.
Arguments:
- states: bfloat16 [256, 3072], P(None, 'seq'), may hold values from -20 to 20
- norm_gain: bfloat16 [3072], P('seq'), may hold values from 0.25 to 1.75
- w_qkv: bfloat16 [3, 3072, 3072], P(None, 'seq', 'tp'), may hold values from -0.109375 to 0.109375
- w_out: bfloat16 [3072, 3072], P('tp', 'seq'), may hold values from -0.109375 to 0.109375
- cache: bfloat16 [768, 2, 64, 3072], P('seq', None, None, 'tp'), may hold values from -400 to 400
- context_len: int32 [256], replicated, may hold values from 1 to 4096, as said below
- block_owner: int32 [768], P('seq'), may hold values from 0 to 256, as said below
- block_index: int32 [768], P('seq'), may hold values from 0 to 63, as said below
Outputs:
- hidden: bfloat16 [256, 3072], P('tp', 'seq')
- updated: bfloat16 [768, 2, 64, 3072], P('seq', None, None, 'tp')
Inputs may be any that keep to these rules, and one draw needn't show every extreme that they name: `context_len`: A request of length n owns exactly ceil(n / 64) pool blocks, with block_index 0, 1, ... once each; at least one pool block is unused. `context_len`: exactly 4 requests own 64/2 blocks or more; every other request owns at most 2 blocks, all on one index of seq. `block_owner`: the value 256 marks an unused block. `block_index`: 0 for an unused block.
All inputs are finite; a program needn't handle non-finite values.
Results may differ from a plain program's by a relative error of at most 0.0068.
Values may be sent and summed in bfloat16 or wider, within the bound.
A program may use at most 128 MiB of HBM per device.

v0:
```python
import jax
import jax.numpy as jnp
from jax import lax
from jax.sharding import PartitionSpec as P

HEAD_DIM = 96
EPSILON = 1e-05
NEG_FLOOR = -1e30


def combined_all(part, axis, combine):
    gathered = jax.tree.map(lambda a: lax.all_gather(a, axis), part)

    def take(source):
        return jax.tree.map(lambda a: lax.dynamic_index_in_dim(a, source, 0, False), gathered)

    return lax.fori_loop(
        1, lax.axis_size(axis), lambda source, state: combine(state, take(source)), take(0)
    )


def rotate(values, positions):
    half_dim = HEAD_DIM // 2
    frequency = 10000.0 ** (-jnp.arange(half_dim, dtype=jnp.float32) * 2.0 / HEAD_DIM)
    angles = positions.astype(jnp.float32)[:, None] * frequency[None, :]
    cosine = jnp.cos(angles)[:, None, :]
    sine_part = jnp.sin(angles)[:, None, :]
    front_half = values[..., :half_dim]
    back_half = values[..., half_dim:]
    return jnp.concatenate(
        [front_half * cosine - back_half * sine_part, back_half * cosine + front_half * sine_part],
        axis=-1,
    )


def finish(projected, positions):
    row_count = projected.shape[0]
    columns = projected.shape[2]
    head_count = columns // HEAD_DIM
    query = rotate(
        projected[:, 0].reshape(row_count, head_count, HEAD_DIM), positions
    ) * HEAD_DIM ** (-0.5)
    keys_new = rotate(projected[:, 1].reshape(row_count, head_count, HEAD_DIM), positions)
    return (
        query.astype(jnp.bfloat16).reshape(row_count, columns),
        keys_new.astype(jnp.bfloat16).reshape(row_count, columns),
        projected[:, 2].astype(jnp.bfloat16),
    )


def join(earlier, later):
    highest = jnp.maximum(earlier[0], later[0])
    left_scale = jnp.exp(earlier[0] - highest)
    right_scale = jnp.exp(later[0] - highest)
    return (
        highest,
        earlier[1] * left_scale + later[1] * right_scale,
        earlier[2] * jnp.repeat(left_scale, HEAD_DIM, axis=1)
        + later[2] * jnp.repeat(right_scale, HEAD_DIM, axis=1),
    )


def shards(states, norm_gain, w_qkv, w_out, cache, context_len, block_owner, block_index):
    requests = states.shape[0]
    seq_count = lax.axis_size("seq")
    wide_states = states.astype(jnp.float32)
    sum_squares = lax.psum(jnp.sum(wide_states * wide_states, axis=1), "seq")
    inverse = lax.rsqrt(sum_squares / (states.shape[1] * seq_count) + EPSILON)
    normed = (wide_states * inverse[:, None] * norm_gain.astype(jnp.float32)[None, :]).astype(
        jnp.bfloat16
    )
    positions = context_len - 1
    local_term = jnp.einsum("rd,cdh->rch", normed, w_qkv, preferred_element_type=jnp.float32)
    projected = lax.psum(local_term, "seq")
    query, keys_new, values_new = finish(projected, positions)
    blocks, _, tokens, columns = cache.shape
    head_count = columns // HEAD_DIM
    block_live = block_owner < requests
    owner_row = jnp.minimum(block_owner, requests - 1)
    last_position = positions[owner_row]
    block_hit = block_live & (block_index == last_position // tokens)
    slot_hit = block_hit[:, None] & (
        jnp.arange(tokens, dtype=jnp.int32)[None, :] == (last_position % tokens)[:, None]
    )
    fresh_rows = jnp.stack([keys_new[owner_row], values_new[owner_row]], axis=1)
    updated = jnp.where(slot_hit[:, None, :, None], fresh_rows[:, :, None, :], cache)
    query_rows = query[owner_row].reshape(blocks, head_count, HEAD_DIM)
    key_cache = updated[:, 0].reshape(blocks, tokens, head_count, HEAD_DIM)
    value_cache = updated[:, 1].reshape(blocks, tokens, head_count, HEAD_DIM)
    scores = jnp.einsum("bhd,bthd->bht", query_rows, key_cache, preferred_element_type=jnp.float32)
    token_position = block_index[:, None] * tokens + jnp.arange(tokens, dtype=jnp.int32)[None, :]
    visible = block_live[:, None] & (token_position < context_len[owner_row][:, None])
    masked = jnp.where(visible[:, None, :], scores, NEG_FLOOR)
    block_max = jnp.max(masked, axis=-1)
    weights = jnp.where(visible[:, None, :], jnp.exp(masked - block_max[..., None]), 0.0).astype(
        jnp.bfloat16
    )
    block_sum = jnp.sum(weights.astype(jnp.float32), axis=-1)
    block_out = jnp.einsum(
        "bht,bthd->bhd", weights, value_cache, preferred_element_type=jnp.float32
    ).reshape(blocks, columns)
    segment = jnp.where(block_live, block_owner, requests)
    member = segment[None, :] == jnp.arange(requests, dtype=jnp.int32)[:, None]
    local_max = jnp.max(jnp.where(member[:, :, None], block_max[None, :, :], NEG_FLOOR), axis=1)
    factor = jnp.exp(block_max - local_max[owner_row])
    member_matrix = member.astype(jnp.float32)
    totals = jnp.dot(member_matrix, block_sum * factor, precision=lax.Precision.HIGHEST)
    outputs = jnp.dot(
        member_matrix,
        block_out * jnp.repeat(factor, HEAD_DIM, axis=1),
        precision=lax.Precision.HIGHEST,
    )
    merged = combined_all((local_max, totals, outputs), "seq", join)
    attended = (merged[2] / jnp.repeat(merged[1], HEAD_DIM, axis=1)).astype(jnp.bfloat16)
    terms = jnp.dot(attended, w_out, preferred_element_type=jnp.float32)
    summed = lax.psum_scatter(terms, "tp", scatter_dimension=0, tiled=True)
    row_count = summed.shape[0]
    residual_rows = lax.dynamic_slice_in_dim(
        wide_states, lax.axis_index("tp") * row_count, row_count, 0
    )
    hidden = (summed + residual_rows).astype(jnp.bfloat16)
    return (hidden, updated)


def solution(mesh):
    return jax.shard_map(
        shards,
        mesh=mesh,
        in_specs=(
            P(None, "seq"),
            P("seq"),
            P(None, "seq", "tp"),
            P("tp", "seq"),
            P("seq", None, None, "tp"),
            P(),
            P("seq"),
            P("seq"),
        ),
        out_specs=(P("tp", "seq"), P("seq", None, None, "tp")),
        check_vma=False,
    )
```

profile of v0, /device:TPU:0, one launch (start us, length us, event | category | flops | bytes accessed | tf_op | source)
XLA Modules:
  0.0 399.5 jit_solution(8305740966183515385)
XLA Ops:
  7.2 0.9 multiply_reduce_fusion
  8.1 68.7 %psum.14 = f32[256]{0:T(256)S(1)} all-reduce(f32[256]{0:T(256)S(1)} %multiply_reduce_fusion), channel_id=1, replica_groups=mesh['seq'=32,'tp'=4] {'seq'}, use_global_device_ids=true, to_apply=%region_1.0 | all-reduce | flops 256 | bytes 2048 | tf_op jit(solution)/shard_map/psum | solution.py:67
  76.8 0.7 convert_element_type.43
  77.5 2.8 fusion.12
  80.4 0.7 gather_fusion
  81.1 0.7 gather_fusion.2
  82.3 102.0 %all-reduce.2.cloned.1.call-done = f32[256,3,768]{2,0,1:T(8,128)} async-done(((f32[256,3,768]{2,0,1:T(8,128)}), f32[256,3,768]{2,0,1:T(8,128)}) %all-reduce.2.cloned.1.call-update) | async-done | bytes 2359312 | tf_op jit(solution)/shard_map/psum | solution.py:74
  184.3 1.5 fusion.28
  186.3 1.1 subtract_convert_fusion
  187.6 0.6 gather_fusion.3
  188.2 1.2 fusion.9
  189.4 0.6 gather_fusion.4
  190.1 2.7 broadcast_select_fusion
  192.8 2.2 fusion.27
  195.0 0.7 copy-done.2
  195.7 6.4 %reshape_squeeze.14 = bf16[24,64,8,96]{3,2,1,0:T(8,128)(2,1)} reshape(bf16[24,1,64,768]{3,2,1,0:T(8,128)(2,1)} %get-tuple-element.239) | data formatting | bytes 4718592 | tf_op jit(solution)/shard_map/reshape;squeeze | solution.py:88
  202.2 1.2 fusion.7
  203.3 0.9 copy.50
  204.3 1.7 gather_fusion.1
  206.1 3.6 fusion.5
  210.0 4.3 %reshape_squeeze.15 = bf16[24,64,8,96]{3,2,1,0:T(8,128)(2,1)} reshape(bf16[24,1,64,768]{3,2,1,0:T(8,128)(2,1)S(1)} %get-tuple-element.238) | data formatting | bytes 4718592 | tf_op jit(solution)/shard_map/reshape;squeeze | solution.py:89
  214.5 0.6 gather_fusion.5
  215.1 2.8 fusion.3
  218.1 1.5 fusion.17
  219.9 25.3 %all-gather.1 = f32[8192,8]{0,1:T(8,128)S(1)} all-gather(f32[256,8]{0,1:T(8,128)S(1)} %fusion.18), channel_id=3, replica_groups=mesh['seq'=32,'tp'=4] {'seq'}, dimensions={0}, use_global_device_ids=true | all-gather | bytes 270336 | tf_op jit(solution)/shard_map/all_gather | solution.py:12
  245.2 22.3 %all-gather = f32[8192,8]{0,1:T(8,128)S(1)} all-gather(f32[256,8]{0,1:T(8,128)S(1)} %select_reduce_fusion), channel_id=2, replica_groups=mesh['seq'=32,'tp'=4] {'seq'}, dimensions={0}, use_global_device_ids=true | all-gather | bytes 270336 | tf_op jit(solution)/shard_map/all_gather | solution.py:12
  267.5 44.9 %all-gather.5.cloned.1.call-done = f32[8192,768]{1,0:T(8,128)} async-done(((f32[256,768]{1,0:T(8,128)}), f32[8192,768]{1,0:T(8,128)}) %all-gather.5.cloned.1.call-update) | async-done | bytes 25165840 | tf_op jit(solution)/shard_map/all_gather | solution.py:12
  312.5 1.2 slice.66
  313.9 56.6 %while.19 = (s32[]{:T(128)}, f32[256,8]{0,1:T(8,128)S(1)}, f32[256,8]{0,1:T(8,128)S(1)}, f32[256,768]{0,1:T(8,128)S(1)}, f32[32,256,8]{1,2,0:T(8,128)S(1)}, /*in...) while((s32[]{:T(128)}, f32[256,8]{0,1:T(8,128)S(1)}, ...), condition=%wide.region_7.8_spmd, body=%wide.region_6.7_spmd.sunk | while | flops 602117 | bytes 5587095 | solution.py:17
  314.0 1.2 constant_dynamic-slice_fusion.2
  315.8 1.2 constant_dynamic-slice_fusion.2
  317.7 1.2 constant_dynamic-slice_fusion.2
  319.5 1.2 constant_dynamic-slice_fusion.2
  321.3 1.2 constant_dynamic-slice_fusion.2
  323.1 1.2 constant_dynamic-slice_fusion.2
  325.0 1.2 constant_dynamic-slice_fusion.2
  326.8 1.2 constant_dynamic-slice_fusion.2
  328.6 1.2 constant_dynamic-slice_fusion.2
  330.4 1.2 constant_dynamic-slice_fusion.2
  332.2 1.2 constant_dynamic-slice_fusion.2
  334.1 1.2 constant_dynamic-slice_fusion.2
  335.9 1.2 constant_dynamic-slice_fusion.2
  337.7 1.2 constant_dynamic-slice_fusion.2
  339.5 1.2 constant_dynamic-slice_fusion.2
  341.4 1.2 constant_dynamic-slice_fusion.2
  343.2 1.2 constant_dynamic-slice_fusion.2
  345.0 1.2 constant_dynamic-slice_fusion.2
  346.8 1.2 constant_dynamic-slice_fusion.2
  348.7 1.2 constant_dynamic-slice_fusion.2
  350.5 1.2 constant_dynamic-slice_fusion.2
  352.3 1.2 constant_dynamic-slice_fusion.2
  354.1 1.2 constant_dynamic-slice_fusion.2
  356.0 1.2 constant_dynamic-slice_fusion.2
  357.8 1.2 constant_dynamic-slice_fusion.2
  359.6 1.2 constant_dynamic-slice_fusion.2
  361.4 1.2 constant_dynamic-slice_fusion.2
  363.3 1.2 constant_dynamic-slice_fusion.2
  365.1 1.2 constant_dynamic-slice_fusion.2
  366.9 1.2 constant_dynamic-slice_fusion.2
  368.7 1.2 constant_dynamic-slice_fusion.2
  370.6 1.0 fusion.29
  371.6 19.7 %reduce-scatter.4.cloned.1.call-done = f32[64,96]{1,0:T(8,128)} async-done(((f32[256,96]{1,0:T(8,128)}), f32[64,96]{1,0:T(8,128)}) %reduce-scatter.4.cloned.1.call-update) | async-done | bytes 24592
  391.3 0.8 copy.67
  392.3 0.7 copy.58
  (144 shorter events, 21.4 us)
Async XLA Ops:
  7.2 70.3 %copy-start = (bf16[3,96,768]{2,1,0:T(8,128)(2,1)S(1)}, bf16[3,96,768]{2,1,0:T(8,128)(2,1)}, u32[]{:S(2)}) copy-start(bf16[3,96,768]{2,1,0:T(8,128)(2,1)} %param.12) | copy-start | bytes 1327108
  7.2 73.1 %copy-start.1 = (s32[256]{0:T(256)S(1)}, s32[256]{0:T(256)}, u32[]{:S(2)}) copy-start(s32[256]{0:T(256)} %param.15) | copy-start | bytes 3076
  7.2 73.1 %copy-start.5 = (s32[24]{0:T(128)S(1)}, s32[24]{0:T(128)}, u32[]{:S(2)}) copy-start(s32[24]{0:T(128)} %param.16) | copy-start | bytes 292
  7.2 177.1 %all-reduce.2.cloned.1.call-start = ((), (), s32[]{:S(2)}) async-start(), calls=%async_computation.1 | async-start | bytes 4718592 | tf_op jit(solution)/shard_map/psum | solution.py:74
  8.1 73.7 %copy-start.6 = (s32[24]{0:T(128)S(1)}, s32[24]{0:T(128)}, u32[]{:S(2)}) copy-start(s32[24]{0:T(128)} %param.17) | copy-start | bytes 292
  80.3 232.2 %all-gather.5.cloned.1.call-start = ((), (), s32[]{:S(2)}) async-start(), calls=%async_computation.2 | async-start | bytes 25952256 | tf_op jit(solution)/shard_map/all_gather | solution.py:12
  192.8 2.9 copy-start.2
  219.7 171.6 %reduce-scatter.4.cloned.1.call-start = ((), (), s32[]{:S(2)}) async-start(), calls=%async_computation.3 | async-start | bytes 163840
  313.9 56.7 %copy-start.4 = (bf16[768,96]{0,1:T(8,128)(2,1)S(1)}, bf16[768,96]{0,1:T(8,128)(2,1)}, u32[]{:S(2)}) copy-start(bf16[768,96]{0,1:T(8,128)(2,1)} %param.13) | copy-start | bytes 442372
  313.9 57.7 %copy-start.3 = (bf16[256,96]{0,1:T(8,128)(2,1)S(1)}, bf16[256,96]{0,1:T(8,128)(2,1)}, u32[]{:S(2)}) copy-start(bf16[256,96]{0,1:T(8,128)(2,1)} %param.10) | copy-start | bytes 147460
Sparse Core Ops, SparseCore 0:
  80.4 103.8 all-reduce.1
  219.8 92.5 all-gather.4
  371.7 19.5 reduce-scatter.3
where the time goes:
time: 402 us; the launch traced here: 399 us
  waiting for transfers between devices  167 us (42%)
  blocking collectives  116 us (29%)
  local copies, waits for them, and re-layouts  71.3 us (18%)
  other arithmetic  18 us (4%)
  between operations  14.1 us (4%)
  matrix products  11.8 us (3%)
    psum x1, waiting for transfers between devices, shards(): projected = lax.psum(local_term, 'seq')  102 us
    psum x1, blocking collectives, shards(): sum_squares = lax.psum(jnp.sum(wide_states * wide_states, axis=1), 'seq')  68.7 us
    all_gather x2, blocking collectives, combined_all(): gathered = jax.tree.map(lambda a: lax.all_gather(a, axis), part)  47.6 us
    dynamic_slice x65, local copies, waits for them, and re-layouts, take(): lax.dynamic_index_in_dim(a, source, 0, False)  46.3 us
    all_gather x1, waiting for transfers between devices, combined_all(): gathered = jax.tree.map(lambda a: lax.all_gather(a, axis), part)  44.9 us
    unnamed x4, waiting for transfers between devices  19.8 us
    add x31, other arithmetic, join(): earlier[2] * jnp.repeat(left_scale, HEAD_DIM, axis=1)  9.66 us
  transfers between devices with their start and end apart: 3, of which 3 were waited for; matrix products, arithmetic and copies ran while one was open for 1% of the time, Pallas kernels for 0%

commit v1 on v0

--- a/solution.py
+++ b/solution.py
@@ -71,7 +71,11 @@
     )
     positions = context_len - 1
     local_term = jnp.einsum("rd,cdh->rch", normed, w_qkv, preferred_element_type=jnp.float32)
-    projected = lax.psum(local_term, "seq")
+    projected = local_term
+    for hop in (1, 2, 4, 8, 16):
+        projected = projected + lax.ppermute(
+            projected, "seq", [(dev, dev ^ hop) for dev in range(32)]
+        )
     query, keys_new, values_new = finish(projected, positions)
     blocks, _, tokens, columns = cache.shape
     head_count = columns // HEAD_DIM

time: 402 us -> 509 us (1.27)
  waiting for transfers between devices: 167 us -> 276 us
    ppermute x0 -> x5, waiting for transfers between devices: none -> 214 us  [shards(): lax.ppermute(projected, 'seq', [(dev, dev ^ hop) for dev in range(32)])]
    psum x1 -> x0, waiting for transfers between devices: 102 us -> none  [shards(): projected = lax.psum(local_term, 'seq')]
    unnamed x4 -> x3, waiting for transfers between devices: 19.8 us -> 19.8 us
  transfers between devices with their start and end apart: 3 -> 7, of which waited for: 3 -> 7; matrix products, arithmetic and copies ran while one was open for 1% -> 0% of each run, Pallas kernels for 0% -> 0%
where the time goes in v1:
time: 509 us; the launch traced here: 507 us
  waiting for transfers between devices  276 us (54%)
  blocking collectives  116 us (23%)
  local copies, waits for them, and re-layouts  67.8 us (13%)
  other arithmetic  20.8 us (4%)
  between operations  14.5 us (3%)
  matrix products  10.5 us (2%)
    ppermute x5, waiting for transfers between devices, shards(): lax.ppermute(projected, 'seq', [(dev, dev ^ hop) for dev in range(32)])  214 us
    psum x1, blocking collectives, shards(): sum_squares = lax.psum(jnp.sum(wide_states * wide_states, axis=1), 'seq')  68.7 us
    all_gather x2, blocking collectives, combined_all(): gathered = jax.tree.map(lambda a: lax.all_gather(a, axis), part)  46.9 us
    dynamic_slice x65, local copies, waits for them, and re-layouts, take(): lax.dynamic_index_in_dim(a, source, 0, False)  46.3 us
    all_gather x1, waiting for transfers between devices, combined_all(): gathered = jax.tree.map(lambda a: lax.all_gather(a, axis), part)  43.1 us
    unnamed x3, waiting for transfers between devices  19.8 us
  transfers between devices with their start and end apart: 7, of which 7 were waited for; matrix products, arithmetic and copies ran while one was open for 0% of the time, Pallas kernels for 0%

profile of v1, /device:TPU:0, one launch (start us, length us, event | category | flops | bytes accessed | tf_op | source)
XLA Modules:
  0.0 507.2 jit_solution(3845944303299470930)
XLA Ops:
  7.2 0.9 multiply_reduce_fusion
  8.1 68.7 %psum.7 = f32[256]{0:T(256)S(1)} all-reduce(f32[256]{0:T(256)S(1)} %multiply_reduce_fusion), channel_id=1, replica_groups=mesh['seq'=32,'tp'=4] {'seq'}, use_global_device_ids=true, to_apply=%region_1.0 | all-reduce | flops 256 | bytes 2048 | tf_op jit(solution)/shard_map/psum | solution.py:67
  76.8 0.7 convert_element_type.43
  77.4 1.4 fusion.12
  78.9 4.5 collective-permute-done
  83.8 53.3 %collective-permute-done.1 = f32[256,3,768]{2,0,1:T(8,128)S(1)} collective-permute-done((f32[256,3,768]{2,0,1:T(8,128)S(1)}, f32[256,3,768]{2,0,1:T(8,128)S(1)}, u32[]{:S(2)}, u32[]{:S(2)}) %collective-permute-start.1) | collective-permute-done | bytes 2359328 | tf_op jit(solution)/shard_map/ppermute | solution.py:76
  137.5 54.0 %collective-permute-done.2 = f32[256,3,768]{2,0,1:T(8,128)S(1)} collective-permute-done((f32[256,3,768]{2,0,1:T(8,128)S(1)}, f32[256,3,768]{2,0,1:T(8,128)S(1)}, u32[]{:S(2)}, u32[]{:S(2)}) %collective-permute-start.2) | collective-permute-done | bytes 2359328 | tf_op jit(solution)/shard_map/ppermute | solution.py:76
  191.8 52.2 %collective-permute-done.3 = f32[256,3,768]{2,0,1:T(8,128)S(1)} collective-permute-done((f32[256,3,768]{2,0,1:T(8,128)S(1)}, f32[256,3,768]{2,0,1:T(8,128)S(1)}, u32[]{:S(2)}, u32[]{:S(2)}) %collective-permute-start.3) | collective-permute-done | bytes 2359328 | tf_op jit(solution)/shard_map/ppermute | solution.py:76
  244.5 0.7 gather_fusion
  245.2 0.7 gather_fusion.2
  246.4 49.6 %collective-permute-done.4 = f32[256,3,768]{2,0,1:T(8,128)} collective-permute-done((f32[256,3,768]{2,0,1:T(8,128)S(1)}, f32[256,3,768]{2,0,1:T(8,128)}, u32[]{:S(2)}, u32[]{:S(2)}) %collective-permute-start.4) | collective-permute-done | bytes 2359328 | tf_op jit(solution)/shard_map/ppermute | solution.py:76
  296.0 2.0 add.146
  298.0 0.8 fusion.9
  299.4 1.0 subtract_convert_fusion
  300.5 0.6 gather_fusion.3
  301.8 2.7 broadcast_select_fusion
  304.6 2.2 fusion.27
  306.8 0.7 copy-done.3
  307.5 6.4 %reshape_squeeze.14 = bf16[24,64,8,96]{3,2,1,0:T(8,128)(2,1)} reshape(bf16[24,1,64,768]{3,2,1,0:T(8,128)(2,1)} %get-tuple-element.239) | data formatting | bytes 4718592 | tf_op jit(solution)/shard_map/reshape;squeeze | solution.py:92
  313.9 1.1 fusion.7
  315.9 3.6 fusion.5
  319.8 4.4 reshape_squeeze.15
  325.0 2.8 fusion.3
  328.0 1.6 fusion.17
  329.8 23.3 %all-gather.1 = f32[8192,8]{0,1:T(8,128)S(1)} all-gather(f32[256,8]{0,1:T(8,128)S(1)} %fusion.18), channel_id=3, replica_groups=mesh['seq'=32,'tp'=4] {'seq'}, dimensions={0}, use_global_device_ids=true | all-gather | bytes 270336 | tf_op jit(solution)/shard_map/all_gather | solution.py:12
  353.1 23.6 %all-gather = f32[8192,8]{0,1:T(8,128)S(1)} all-gather(f32[256,8]{0,1:T(8,128)S(1)} %select_reduce_fusion), channel_id=2, replica_groups=mesh['seq'=32,'tp'=4] {'seq'}, dimensions={0}, use_global_device_ids=true | all-gather | bytes 270336 | tf_op jit(solution)/shard_map/all_gather | solution.py:12
  376.7 43.1 %all-gather.5.cloned.1.call-done = f32[8192,768]{1,0:T(8,128)} async-done(((f32[256,768]{1,0:T(8,128)}), f32[8192,768]{1,0:T(8,128)}) %all-gather.5.cloned.1.call-update) | async-done | bytes 25165840 | tf_op jit(solution)/shard_map/all_gather | solution.py:12
  419.8 1.2 slice.66
  421.3 56.6 %while.19 = (s32[]{:T(128)}, f32[256,8]{0,1:T(8,128)S(1)}, f32[256,8]{0,1:T(8,128)S(1)}, f32[256,768]{0,1:T(8,128)S(1)}, f32[32,256,8]{1,2,0:T(8,128)S(1)}, /*in...) while((s32[]{:T(128)}, f32[256,8]{0,1:T(8,128)S(1)}, ...), condition=%wide.region_6.7_spmd, body=%wide.region_5.6_spmd.sunk | while | flops 602117 | bytes 5587095 | solution.py:17
  421.3 1.2 constant_dynamic-slice_fusion.2
  423.2 1.2 constant_dynamic-slice_fusion.2
  425.0 1.2 constant_dynamic-slice_fusion.2
  426.8 1.2 constant_dynamic-slice_fusion.2
  428.6 1.2 constant_dynamic-slice_fusion.2
  430.5 1.2 constant_dynamic-slice_fusion.2
  432.3 1.2 constant_dynamic-slice_fusion.2
  434.1 1.2 constant_dynamic-slice_fusion.2
  435.9 1.2 constant_dynamic-slice_fusion.2
  437.7 1.2 constant_dynamic-slice_fusion.2
  439.6 1.2 constant_dynamic-slice_fusion.2
  441.4 1.2 constant_dynamic-slice_fusion.2
  443.2 1.2 constant_dynamic-slice_fusion.2
  445.0 1.2 constant_dynamic-slice_fusion.2
  446.9 1.2 constant_dynamic-slice_fusion.2
  448.7 1.2 constant_dynamic-slice_fusion.2
  450.5 1.2 constant_dynamic-slice_fusion.2
  452.3 1.2 constant_dynamic-slice_fusion.2
  454.2 1.2 constant_dynamic-slice_fusion.2
  456.0 1.2 constant_dynamic-slice_fusion.2
  457.8 1.2 constant_dynamic-slice_fusion.2
  459.6 1.2 constant_dynamic-slice_fusion.2
  461.5 1.2 constant_dynamic-slice_fusion.2
  463.3 1.2 constant_dynamic-slice_fusion.2
  465.1 1.2 constant_dynamic-slice_fusion.2
  466.9 1.2 constant_dynamic-slice_fusion.2
  468.8 1.2 constant_dynamic-slice_fusion.2
  470.6 1.2 constant_dynamic-slice_fusion.2
  472.4 1.2 constant_dynamic-slice_fusion.2
  474.2 1.2 constant_dynamic-slice_fusion.2
  476.1 1.2 constant_dynamic-slice_fusion.2
  477.9 1.0 fusion.29
  479.0 19.8 %reduce-scatter.4.cloned.1.call-done = f32[64,96]{1,0:T(8,128)} async-done(((f32[256,96]{1,0:T(8,128)}), f32[64,96]{1,0:T(8,128)}) %reduce-scatter.4.cloned.1.call-update) | async-done | bytes 24592
  498.7 0.8 copy.67
  499.7 0.7 copy.58
  (160 shorter events, 24.9 us)
Async XLA Ops:
  7.2 70.3 %copy-start = (bf16[3,96,768]{2,1,0:T(8,128)(2,1)S(1)}, bf16[3,96,768]{2,1,0:T(8,128)(2,1)}, u32[]{:S(2)}) copy-start(bf16[3,96,768]{2,1,0:T(8,128)(2,1)} %param.12) | copy-start | bytes 1327108
  7.2 412.6 %all-gather.5.cloned.1.call-start = ((), (), s32[]{:S(2)}) async-start(), calls=%async_computation.1 | async-start | bytes 25952256 | tf_op jit(solution)/shard_map/all_gather | solution.py:12
  78.8 4.6 collective-permute-start
  83.7 53.4 %collective-permute-start.1 = (f32[256,3,768]{2,0,1:T(8,128)S(1)}, f32[256,3,768]{2,0,1:T(8,128)S(1)}, u32[]{:S(2)}, u32[]{:S(2)}) collective-permute-start(f32[256,3,768]{2,0,1:T(8,128)S(1)} %add.142), channel_id=1, source_target_pairs={{0,8},{4,12},{8,0},{12,4},{16,24},{20,28},{24,16},{28,20},{32,40},... | collective-permute-start | bytes 7077896 | tf_op jit(solution)/shard_map/ppermute | solution.py:76
  137.4 54.0 %collective-permute-start.2 = (f32[256,3,768]{2,0,1:T(8,128)S(1)}, f32[256,3,768]{2,0,1:T(8,128)S(1)}, u32[]{:S(2)}, u32[]{:S(2)}) collective-permute-start(f32[256,3,768]{2,0,1:T(8,128)S(1)} %add.143), channel_id=1, source_target_pairs={{0,16},{4,20},{8,24},{12,28},{16,0},{20,4},{24,8},{28,12},{32,48},... | collective-permute-start | bytes 7077896 | tf_op jit(solution)/shard_map/ppermute | solution.py:76
  191.7 52.7 %copy-start.7 = (s32[24]{0:T(128)S(1)}, s32[24]{0:T(128)}, u32[]{:S(2)}) copy-start(s32[24]{0:T(128)} %param.16) | copy-start | bytes 292
  191.7 52.7 %copy-start.2 = (s32[256]{0:T(256)S(1)}, s32[256]{0:T(256)}, u32[]{:S(2)}) copy-start(s32[256]{0:T(256)} %param.15) | copy-start | bytes 3076
  191.7 54.2 %copy-start.8 = (s32[24]{0:T(128)S(1)}, s32[24]{0:T(128)}, u32[]{:S(2)}) copy-start(s32[24]{0:T(128)} %param.17) | copy-start | bytes 292
  191.7 52.3 %collective-permute-start.3 = (f32[256,3,768]{2,0,1:T(8,128)S(1)}, f32[256,3,768]{2,0,1:T(8,128)S(1)}, u32[]{:S(2)}, u32[]{:S(2)}) collective-permute-start(f32[256,3,768]{2,0,1:T(8,128)S(1)} %add.144), channel_id=1, source_target_pairs={{0,32},{4,36},{8,40},{12,44},{16,48},{20,52},{24,56},{28,60},{32,0... | collective-permute-start | bytes 7077896 | tf_op jit(solution)/shard_map/ppermute | solution.py:76
  244.3 51.6 %collective-permute-start.4 = (f32[256,3,768]{2,0,1:T(8,128)S(1)}, f32[256,3,768]{2,0,1:T(8,128)}, u32[]{:S(2)}, u32[]{:S(2)}) collective-permute-start(f32[256,3,768]{2,0,1:T(8,128)S(1)} %add.145), channel_id=1, source_target_pairs={{0,64},{4,68},{8,72},{12,76},{16,80},{20,84},{24,88},{28,92},{32,9... | collective-permute-start | bytes 7077896 | tf_op jit(solution)/shard_map/ppermute | solution.py:76
  299.4 1.8 copy-start.4
  304.6 2.9 copy-start.3
  329.6 169.2 %reduce-scatter.4.cloned.1.call-start = ((), (), s32[]{:S(2)}) async-start(), calls=%async_computation.2 | async-start | bytes 163840
  421.2 56.7 %copy-start.6 = (bf16[768,96]{0,1:T(8,128)(2,1)S(1)}, bf16[768,96]{0,1:T(8,128)(2,1)}, u32[]{:S(2)}) copy-start(bf16[768,96]{0,1:T(8,128)(2,1)} %param.13) | copy-start | bytes 442372
  421.3 57.7 %copy-start.5 = (bf16[256,96]{0,1:T(8,128)(2,1)S(1)}, bf16[256,96]{0,1:T(8,128)(2,1)}, u32[]{:S(2)}) copy-start(bf16[256,96]{0,1:T(8,128)(2,1)} %param.10) | copy-start | bytes 147460
  477.8 22.5 %copy-start.1 = (bf16[3,96,768]{2,1,0:T(8,128)(2,1)S(1)}, bf16[3,96,768]{2,1,0:T(8,128)(2,1)}, u32[]{:S(2)}) copy-start(bf16[3,96,768]{2,1,0:T(8,128)(2,1)} %param.12) | copy-start | bytes 1327108
Sparse Core Ops, SparseCore 0:
  329.7 90.0 all-gather.4
  479.0 19.6 reduce-scatter.3
